TPU v7x, 256 devices: a whole 4x4x8 slice. The times are simulated.
256 devices in a mesh: req: 16 (over z, core), mp: 16 (over x, y).
Axes of the slice: x: 4, y: 4, z: 8, core: 2. Of those that a mesh axis runs over, the one named last changes fastest.
Arguments:
- tokens_in: bfloat16 [2048, 2048], P('req', 'mp'), may hold values from -6 to 6
- req_lengths: int32 [16, 4], replicated, may hold values from 1 to 64, 128 in all within a row
- req_groups: int32 [16, 4], replicated, may hold values from 0 to 1
- prefix_cache: bfloat16 [2, 4096, 2, 2048], P(None, 'req', None, 'mp'), may hold values from -170 to 170, as said below
- attn_gain: bfloat16 [2048], replicated, may hold values from 0.25 to 1.75
- mlp_gain: bfloat16 [2048], replicated, may hold values from 0.25 to 1.75
- w_qkv: bfloat16 [2048, 3, 2048], P(None, None, 'mp'), may hold values from -0.25 to 0.25
- w_out: bfloat16 [2048, 2048], P('mp'), may hold values from -0.1875 to 0.1875
- w_gate_up: bfloat16 [2048, 2, 5632], P(None, None, 'mp'), may hold values from -0.125 to 0.125
- w_down: bfloat16 [5632, 2048], P('mp'), may hold values from -0.109375 to 0.109375
Outputs:
- layer_out: bfloat16 [2048, 2048], P('req', 'mp')
Inputs may be any that keep to these rules, and one draw needn't show every extreme that they name: `req_lengths`: in each row the 4 lengths sum to 128, and the largest is 64. `prefix_cache`: keys are cached after rotation.
All inputs are finite; a program needn't handle non-finite values.
Results may differ from a plain program's by a relative error of at most 0.02.
The roundings to bfloat16 on the way count: a program that leaves them out, or rounds other values in their place, can miss the bound.
Values may be sent and summed in bfloat16 or wider, within the bound.
A program may use at most 64 MiB of HBM per device.

v0:
```python
import jax
import jax.numpy as jnp
from jax import lax
from jax.sharding import PartitionSpec as P

HEAD_DIM = 64
ROT = 16
PREFIX = 4096
GROUPS = 2


NEG = -1e30
EPS = 1e-05


def layer_norm(rows_in, gain_vec):
    values_f = rows_in.astype(jnp.float32)
    row_mean = jnp.mean(values_f, axis=-1, keepdims=True)
    centred = values_f - row_mean
    variance = jnp.mean(centred * centred, axis=-1, keepdims=True)
    return (centred * lax.rsqrt(variance + EPS) * gain_vec.astype(jnp.float32)).astype(jnp.bfloat16)


def rotary(vectors, positions):
    half_rot = ROT // 2
    frequency = 10000.0 ** (-(jnp.arange(half_rot, dtype=jnp.float32) * 2.0 / ROT))
    angles = positions[:, None] * frequency[None, :]
    cosine = jnp.cos(angles)[:, None, :]
    sine_part = jnp.sin(angles)[:, None, :]
    lower_half = vectors[..., :half_rot]
    upper_half = vectors[..., half_rot:ROT]
    return jnp.concatenate(
        [
            lower_half * cosine - upper_half * sine_part,
            upper_half * cosine + lower_half * sine_part,
            vectors[..., ROT:],
        ],
        axis=-1,
    )


def token_meta(length_row, group_row, row_count):
    starts = jnp.cumsum(length_row) - length_row
    places = jnp.arange(row_count, dtype=jnp.int32)
    request = jnp.sum((places[:, None] >= starts[None, :]).astype(jnp.int32), axis=1) - 1
    onehot = (request[:, None] == jnp.arange(length_row.shape[0], dtype=jnp.int32)[None, :]).astype(
        jnp.int32
    )
    offset = places - jnp.sum(onehot * starts[None, :], axis=1)
    groups_of = jnp.sum(onehot * group_row[None, :], axis=1)
    return (request, offset, groups_of)


def combine_states(state_a, state_b):
    mixed_a, top_a, sum_a = state_a
    mixed_b, top_b, sum_b = state_b
    top_new = jnp.maximum(top_a, top_b)
    scale_a = jnp.exp(top_a - top_new)
    scale_b = jnp.exp(top_b - top_new)
    return (
        mixed_a * scale_a[..., None] + mixed_b * scale_b[..., None],
        top_new,
        sum_a * scale_a + sum_b * scale_b,
    )


def rounded_block(query, member, part):
    group_count = part.shape[0]
    block = part.shape[1]
    row_count = query.shape[0]
    heads = query.shape[1]
    key_part = part[:, :, 0].reshape(group_count, block, heads, HEAD_DIM)
    value_part = part[:, :, 1].reshape(group_count * block, heads, HEAD_DIM)
    scores = jnp.einsum(
        "thd,gnhd->htgn", query, key_part, preferred_element_type=jnp.float32
    ) * HEAD_DIM ** (-0.5)
    scores = jnp.where(member[None, :, :, None], scores, NEG).reshape(
        heads, row_count, group_count * block
    )
    top_score = jnp.max(scores, axis=2)
    weights = jnp.exp(scores - top_score[:, :, None])
    weight_sum = jnp.sum(weights, axis=2)
    mixed_out = jnp.einsum(
        "hts,she->the", weights.astype(jnp.bfloat16), value_part, preferred_element_type=jnp.float32
    )
    normed_part = (mixed_out / weight_sum.T[..., None]).astype(jnp.bfloat16)
    return (normed_part, top_score.T, weight_sum.T)


def own_attention(query, keys, values, request, offset):
    scores = jnp.einsum(
        "thd,shd->hts", query, keys, preferred_element_type=jnp.float32
    ) * HEAD_DIM ** (-0.5)
    allowed = (request[:, None] == request[None, :]) & (offset[None, :] <= offset[:, None])
    scores = jnp.where(allowed[None], scores, NEG)
    top_score = jnp.max(scores, axis=2)
    weights = jnp.exp(scores - top_score[:, :, None])
    weight_sum = jnp.sum(weights, axis=2)
    mixed_out = jnp.einsum(
        "hts,she->the", weights.astype(jnp.bfloat16), values, preferred_element_type=jnp.float32
    )
    return (mixed_out, top_score.T, weight_sum.T)


def body(
    tokens_in,
    req_lengths,
    req_groups,
    prefix_cache,
    attn_gain,
    mlp_gain,
    w_qkv,
    w_out,
    w_gate_up,
    w_down,
):
    row_count = tokens_in.shape[0]
    shard_width = tokens_in.shape[1]
    device_row = lax.axis_index("req")
    mp_index = lax.axis_index("mp")
    full_rows = lax.all_gather(tokens_in, "mp", axis=1, tiled=True)
    model_width = full_rows.shape[1]
    normed_attn = layer_norm(full_rows, attn_gain)
    heads = w_qkv.shape[2] // HEAD_DIM
    projected = jnp.dot(
        normed_attn, w_qkv.reshape(model_width, -1), preferred_element_type=jnp.float32
    )
    projected = projected.reshape(row_count, 3, heads, HEAD_DIM)
    length_row = lax.dynamic_index_in_dim(req_lengths, device_row, 0, keepdims=False)
    group_row = lax.dynamic_index_in_dim(req_groups, device_row, 0, keepdims=False)
    request, offset, groups_of = token_meta(length_row, group_row, row_count)
    positions = (PREFIX + offset).astype(jnp.float32)
    query_rot = rotary(projected[:, 0], positions).astype(jnp.bfloat16)
    key_rot = rotary(projected[:, 1], positions).astype(jnp.bfloat16)
    value_rows = projected[:, 2].astype(jnp.bfloat16)
    own_state = own_attention(query_rot, key_rot, value_rows, request, offset)
    group_ids = jnp.arange(GROUPS, dtype=jnp.int32)
    block_rows = prefix_cache.shape[1]
    member = groups_of[:, None] == group_ids[None, :]
    piece = lax.all_gather(prefix_cache, "req", axis=1, tiled=True)

    def step_block(index, carry):
        part = lax.dynamic_slice_in_dim(piece, index * block_rows, block_rows, 1)
        normed_part, part_top, part_sum = rounded_block(query_rot, member, part)
        return combine_states(
            carry, (normed_part.astype(jnp.float32) * part_sum[..., None], part_top, part_sum)
        )

    mixed_out, top_score, weight_sum = lax.fori_loop(
        0, piece.shape[1] // block_rows, step_block, own_state
    )
    attn_rows = (
        (mixed_out / weight_sum[..., None])
        .astype(jnp.bfloat16)
        .reshape(row_count, heads * HEAD_DIM)
    )
    attn_part = jnp.dot(attn_rows, w_out, preferred_element_type=jnp.float32)
    attn_share = lax.psum_scatter(
        attn_part.astype(jnp.bfloat16), "mp", scatter_dimension=1, tiled=True
    ).astype(jnp.float32)
    residual_share = (tokens_in.astype(jnp.float32) + attn_share).astype(jnp.bfloat16)
    residual_f = residual_share.astype(jnp.float32)
    row_sums, row_squares = lax.psum(
        (jnp.sum(residual_f, axis=1), jnp.sum(residual_f * residual_f, axis=1)), "mp"
    )
    row_mean = row_sums / model_width
    variance = row_squares / model_width - row_mean * row_mean
    gain_share = lax.dynamic_slice_in_dim(mlp_gain, mp_index * shard_width, shard_width, 0).astype(
        jnp.float32
    )
    normed_share = (
        (residual_f - row_mean[:, None]) * lax.rsqrt(variance + EPS)[:, None] * gain_share[None, :]
    ).astype(jnp.bfloat16)
    normed_mlp = lax.all_gather(normed_share, "mp", axis=1, tiled=True)
    local_units = w_gate_up.shape[2]
    gate_up = jnp.dot(
        normed_mlp, w_gate_up.reshape(model_width, -1), preferred_element_type=jnp.float32
    ).reshape(row_count, 2, local_units)
    hidden = (jax.nn.silu(gate_up[:, 0]) * gate_up[:, 1]).astype(jnp.bfloat16)
    down_part = jnp.dot(hidden, w_down, preferred_element_type=jnp.float32)
    mlp_share = lax.psum_scatter(
        down_part.astype(jnp.bfloat16), "mp", scatter_dimension=1, tiled=True
    ).astype(jnp.float32)
    return (residual_share.astype(jnp.float32) + mlp_share).astype(jnp.bfloat16)


def solution(mesh):
    return jax.shard_map(
        body,
        mesh=mesh,
        in_specs=(
            P("req", "mp"),
            P(),
            P(),
            P(None, "req", None, "mp"),
            P(),
            P(),
            P(None, None, "mp"),
            P("mp", None),
            P(None, None, "mp"),
            P("mp", None),
        ),
        out_specs=P("req", "mp"),
        check_vma=False,
    )
```

profile of v0, /device:TPU:1, one launch (start us, length us, event | category | flops | bytes accessed | tf_op | source)
XLA Modules:
  0.0 390.1 jit_solution(3455351838395979648)
XLA Ops:
  8.6 2.6 copy.29
  11.2 21.0 %all_gather.9 = bf16[128,2048]{1,0:T(8,128)(2,1)S(1)} all-gather(bf16[128,128]{1,0:T(8,128)(2,1)S(1)} %copy-done.3), channel_id=1, replica_groups=mesh['req'=16,'mp'=16] {'mp'}, dimensions={1}, use_global_device_ids=true | all-gather | bytes 557056 | tf_op jit(solution)/shard_map/all_gather | solution.py:121
  35.9 26.7 %all-gather.2.cloned.1.call-done = bf16[2,4096,2,128]{1,3,0,2:T(8,128)(2,1)} async-done(((bf16[2,256,2,128]{1,3,0,2:T(8,128)(2,1)}), bf16[2,4096,2,128]{1,3,0,2:T(8,128)(2,1)}) %all-gather.2.cloned.1.call-update) | async-done | bytes 4194320 | tf_op jit(solution)/shard_map/all_gather | solution.py:140
  62.6 98.9 %while.18 = (s32[]{:T(128)}, f32[128,2,64]{0,2,1:T(8,128)}, f32[128,2]{0,1:T(2,128)S(1)}, f32[128,2]{0,1:T(2,128)S(1)}, bf16[2,4096,2,128]{1,3,0,2:T(8,128)(2,1)...) while((s32[]{:T(128)}, f32[128,2,64]{0,2,1:T(8,128)}, ...), condition=%wide.region_11.12_spmd.clone, body=%wide.region_8.11_spmd.clone.sunk | while | flops 34587912 | bytes 4112575 | solution.py:149
  66.8 2.0 fusion.64
  73.0 2.0 fusion.64
  79.2 2.0 fusion.64
  85.3 2.0 fusion.64
  91.5 2.0 fusion.64
  97.7 2.0 fusion.64
  103.9 2.0 fusion.64
  110.1 2.0 fusion.64
  116.3 2.0 fusion.64
  122.4 2.0 fusion.64
  128.6 2.0 fusion.64
  134.8 2.0 fusion.64
  141.0 2.0 fusion.64
  147.2 2.0 fusion.64
  153.3 2.0 fusion.64
  159.5 2.0 fusion.64
  165.6 74.0 %reduce-scatter.7.cloned.1.call-done = bf16[128,128]{1,0:T(8,128)(2,1)} async-done(((bf16[2048,128]{1,0:T(8,128)(2,1)}), bf16[128,128]{1,0:T(8,128)(2,1)}) %reduce-scatter.7.cloned.1.call-update) | async-done | bytes 32784
  240.6 30.9 %all-reduce = (f32[128]{0:T(128)S(1)}, f32[128]{0:T(128)S(1)}) all-reduce(f32[128]{0:T(128)S(1)} %get-tuple-element.150, f32[128]{0:T(128)S(1)} %get-tuple-element.149), channel_id=1, replica_groups=mesh['req'=16,'mp'=16] {'mp'}, use_global_device_ids=true, to_apply=%region_16.17 | all-reduce | flops 256 | bytes 2048 | tf_op jit(solution)/shard_map/psum | solution.py:163
  271.6 16.5 %all_gather.11 = bf16[128,2048]{1,0:T(8,128)(2,1)S(1)} all-gather(bf16[128,128]{1,0:T(8,128)(2,1)S(1)} %fusion.37), channel_id=1, replica_groups=mesh['req'=16,'mp'=16] {'mp'}, dimensions={1}, use_global_device_ids=true | all-gather | bytes 557056 | tf_op jit(solution)/shard_map/all_gather | solution.py:174
  291.0 91.1 %reduce-scatter.9.cloned.1.call-done = bf16[128,128]{1,0:T(8,128)(2,1)} async-done(((bf16[2048,128]{1,0:T(8,128)(2,1)}), bf16[128,128]{1,0:T(8,128)(2,1)}) %reduce-scatter.9.cloned.1.call-update) | async-done | bytes 32784
  (188 shorter events, 82.0 us)
Async XLA Ops:
  6.5 281.5 %copy-start = (bf16[2048,2,352]{0,2,1:T(8,128)(2,1)S(1)}, bf16[2048,2,352]{0,2,1:T(8,128)(2,1)}, u32[]{:S(2)}) copy-start(bf16[2048,2,352]{0,2,1:T(8,128)(2,1)} %param.20) | copy-start | bytes 8650756
  6.5 56.1 %all-gather.2.cloned.1.call-start = ((), (), s32[]{:S(2)}) async-start(), calls=%async_computation.2 | async-start | bytes 4456448 | tf_op jit(solution)/shard_map/all_gather | solution.py:140
  8.5 231.0 %reduce-scatter.7.cloned.1.call-start = ((), (), s32[]{:S(2)}) async-start(), calls=%async_computation.3 | async-start | bytes 557056
  8.6 2.6 copy-start.5
  8.6 2.6 copy-start.3
  11.2 21.4 %copy-start.1 = (bf16[2048,3,128]{0,2,1:T(8,128)(2,1)S(1)}, bf16[2048,3,128]{0,2,1:T(8,128)(2,1)}, u32[]{:S(2)}) copy-start(bf16[2048,3,128]{0,2,1:T(8,128)(2,1)} %copy.29) | copy-start | bytes 4718596
  32.7 0.7 copy-start.6
  32.7 0.7 copy-start.7
  161.5 78.9 %copy-start.4 = (bf16[128,128]{1,0:T(8,128)(2,1)S(1)}, bf16[128,128]{1,0:T(8,128)(2,1)}, u32[]{:S(2)}) copy-start(bf16[128,128]{1,0:T(8,128)(2,1)} %param.12) | copy-start | bytes 98308
  164.8 217.3 %reduce-scatter.9.cloned.1.call-start = ((), (), s32[]{:S(2)}) async-start(), calls=%async_computation.4 | async-start | bytes 557056
  288.1 1.4 copy-start.2
Sparse Core Ops, SparseCore 0:
  9.1 53.4 all-gather.1
  164.9 74.6 reduce-scatter.6
  291.1 90.9 reduce-scatter.8
where the time goes:
time: 392 us; the launch traced here: 390 us
  waiting for transfers between devices  192 us (49%)
  blocking collectives  68.4 us (17%)
  matrix products  55.5 us (14%)
  local copies, waits for them, and re-layouts  54.7 us (14%)
  between operations  13.3 us (3%)
  other arithmetic  6.08 us (2%)
    unnamed x5, waiting for transfers between devices  165 us
    dot_general x16, matrix products, rounded_block(): jnp.einsum('hts,she->the', weights.astype(jnp.bfloat16), value_part, pref...  31.8 us
    psum x1, blocking collectives, body(): lax.psum((jnp.sum(residual_f, axis=1), jnp.sum(residual_f * residual_f, a...  30.9 us
    all_gather x1, waiting for transfers between devices, body(): piece = lax.all_gather(prefix_cache, 'req', axis=1, tiled=True)  26.7 us
    slice x16, local copies, waits for them, and re-layouts, rounded_block(): key_part = part[:, :, 0].reshape(group_count, block, heads, HEAD_DIM)  26.1 us
    all_gather x1, blocking collectives, body(): full_rows = lax.all_gather(tokens_in, 'mp', axis=1, tiled=True)  21 us
    dot_general x16, matrix products, rounded_block(): jnp.einsum('thd,gnhd->htgn', query, key_part, preferred_element_type=jnp....  19.2 us
    all_gather x1, blocking collectives, body(): normed_mlp = lax.all_gather(normed_share, 'mp', axis=1, tiled=True)  16.5 us
  transfers between devices with their start and end apart: 3, of which 3 were waited for; matrix products, arithmetic and copies ran while one was open for 2% of the time, Pallas kernels for 0%

commit v1 on v0

v1 whole, which is shorter than its diff:
```python
import functools

import jax
import jax.numpy as jnp
from jax import lax
from jax.experimental import pallas as pl
from jax.experimental.pallas import tpu as pltpu
from jax.sharding import PartitionSpec as P

HEAD_DIM = 64
ROT = 16
PREFIX = 4096
NEG = -1e30
EPS = 1e-05
F32 = jnp.float32
BF16 = jnp.bfloat16
N_MP = 16
N_Z = 8
SIDE = 4
OFFSETS = sorted(
    [(dx, dy) for dx in range(SIDE) for dy in range(SIDE) if (dx, dy) != (0, 0)],
    key=lambda o: (-(min(o[0], SIDE - o[0]) + min(o[1], SIDE - o[1])), o),
)


def dot(a, b, dims=((1,), (0,))):
    return lax.dot_general(a, b, (dims, ((), ())), preferred_element_type=F32)


def layer_kernel(
    lengths, groups, tokens_hbm, prefix_hbm, gain_a_hbm, gain_m_hbm, wqkv_hbm, wout_hbm, wgu_hbm, wdown_hbm,
    out_ref,
    tok, pre, gain_a, gain_m, wqkv, wout, wgu, wdown,
    xf, kv, nrm, p1s, p1r, res, rf, p2s, p2r, q2, acc,
    local_sem, ag1_s, ag1_r, rs1_s, rs1_r, ag2_s, ag2_r, rs2_s, rs2_r, ring_s, ring_r, pair_s, pair_r,
):
    mp = lax.axis_index("mp")
    req = lax.axis_index("req")
    z, core = req // 2, req % 2
    mx, my = mp // SIDE, mp % SIDE

    def at_z(step):
        return lax.rem(z + (step + N_Z), N_Z) * 2 + core

    peers = [lax.rem(mx + dx, SIDE) * SIDE + lax.rem(my + dy, SIDE) for dx, dy in OFFSETS]
    sources = [
        lax.rem(mx + SIDE - dx, SIDE) * SIDE + lax.rem(my + SIDE - dy, SIDE) for dx, dy in OFFSETS
    ]
    right, left, partner = at_z(1), at_z(-1), z * 2 + (1 - core)

    barrier = pltpu.get_barrier_semaphore()
    for near in (right, left, partner):
        pl.semaphore_signal(barrier, inc=1, device_id={"req": near})
    for peer in peers:
        pl.semaphore_signal(barrier, inc=1, device_id={"mp": peer})

    def fetch(index, src, dst):
        copy = pltpu.make_async_copy(src, dst, local_sem.at[index])
        copy.start()
        return copy

    get_pre = fetch(0, prefix_hbm, pre)
    get_tok = fetch(1, tokens_hbm, tok)
    get_ga = fetch(2, gain_a_hbm, gain_a)
    get_gm = fetch(3, gain_m_hbm, gain_m)
    get_qkv = [
        fetch(4 + i, wqkv_hbm.at[i], wqkv.at[:, pl.ds(i * 128, 128)]) for i in range(3)
    ]
    get_out = fetch(7, wout_hbm, wout)
    get_gu = fetch(8, wgu_hbm, wgu)
    get_down = fetch(9, wdown_hbm, wdown)

    rows = kv.shape[2]
    get_pre.wait()
    pick_key = (
        lax.broadcasted_iota(jnp.int32, (2 * rows, rows), 0)
        == 2 * lax.broadcasted_iota(jnp.int32, (2 * rows, rows), 1)
    ).astype(F32).astype(BF16)
    pick_value = (
        lax.broadcasted_iota(jnp.int32, (rows, 2 * rows), 1)
        == 2 * lax.broadcasted_iota(jnp.int32, (rows, 2 * rows), 0) + 1
    ).astype(F32).astype(BF16)
    for g in range(2):
        raw = pre[pl.ds(g * 2 * rows, 2 * rows), :]
        kv[req, 0, pl.ds(g * 128, 128), :] = dot(raw, pick_key, ((0,), (0,))).astype(BF16)
        kv[req, 1, :, pl.ds(g * 128, 128)] = dot(pick_value, raw).astype(BF16)
    get_tok.wait()
    xf[mp] = tok[...]

    pl.semaphore_wait(barrier, 3 + len(OFFSETS))

    def ring_copy(way, hop, part):
        slot = at_z(-hop) if way == 0 else at_z(hop)
        index = way * 8 + hop * 2 + part
        return pltpu.make_async_remote_copy(
            src_ref=kv.at[slot, part], dst_ref=kv.at[slot, part],
            send_sem=ring_s.at[index], recv_sem=ring_r.at[index],
            device_id={"req": right if way == 0 else left},
        )

    def ring_landed(way, hop, part):
        slot = at_z(-hop) if way == 0 else at_z(hop)
        index = way * 8 + (hop - 1) * 2 + part
        return pltpu.make_async_remote_copy(
            src_ref=kv.at[slot, part], dst_ref=kv.at[slot, part],
            send_sem=ring_s.at[index], recv_sem=ring_r.at[index],
            device_id={"req": right if way == 0 else left},
        )

    def pair_copy(pos, slot, part):
        index = pos * 2 + part
        return pltpu.make_async_remote_copy(
            src_ref=kv.at[slot, part], dst_ref=kv.at[slot, part],
            send_sem=pair_s.at[index], recv_sem=pair_r.at[index],
            device_id={"req": partner},
        )

    def pair_landed(pos, slot, part):
        other = slot + 1 - 2 * core
        return pair_copy(pos, other, part)

    sent = []
    for way, part in ((0, 0), (1, 1), (0, 1), (1, 0)):
        copy = ring_copy(way, 0, part)
        copy.start()
        sent.append(copy)
    for part in range(2):
        copy = pair_copy(0, req, part)
        copy.start()
        sent.append(copy)

    def share(src_of, dst, send_sem, recv_sem):
        for n, peer in enumerate(peers):
            copy = pltpu.make_async_remote_copy(
                src_ref=src_of(peer), dst_ref=dst.at[mp],
                send_sem=send_sem.at[n], recv_sem=recv_sem.at[n],
                device_id={"mp": peer},
            )
            copy.start()
            sent.append(copy)

    def landed(n, src_of, dst, send_sem, recv_sem):
        pltpu.make_async_remote_copy(
            src_ref=src_of(peers[n]), dst_ref=dst.at[sources[n]],
            send_sem=send_sem.at[n], recv_sem=recv_sem.at[n],
            device_id={"mp": peers[n]},
        ).wait_recv()

    near_first = list(reversed(range(len(OFFSETS))))

    share(lambda peer: tok, xf, ag1_s, ag1_r)

    def service(hop):
        for way, part in ((0, 0), (1, 1), (0, 1), (1, 0)):
            if hop == 4 and way != part:
                continue
            ring_landed(way, hop, part).wait_recv()
            if hop < 3 or (hop == 3 and way == part):
                copy = ring_copy(way, hop, part)
                copy.start()
                sent.append(copy)
            slot = at_z(-hop) if way == 0 else at_z(hop)
            copy = pair_copy(hop if way == 0 else 4 + hop, slot, part)
            copy.start()
            sent.append(copy)

    starts = []
    total = jnp.int32(0)
    for r in range(4):
        starts.append(total)
        total = total + lengths[r, req]

    def meta(shape, axis):
        place = lax.broadcasted_iota(jnp.int32, shape, axis)
        request = jnp.zeros(shape, jnp.int32)
        start = jnp.zeros(shape, jnp.int32)
        group = jnp.full(shape, groups[0, req], jnp.int32)
        for r in range(1, 4):
            inside = place >= starts[r]
            request = request + inside.astype(jnp.int32)
            start = jnp.where(inside, starts[r], start)
            group = jnp.where(inside, groups[r, req], group)
        return place, request, place - start, group

    square = (128, 128)
    row_place, row_request, row_offset, row_group = meta(square, 0)
    col_place, col_request, _, _ = meta(square, 1)
    allowed = (row_request == col_request) & (col_place <= row_place)
    lane = lax.broadcasted_iota(jnp.int32, square, 1)
    in_head = lax.rem(lane, HEAD_DIM)
    pair = lax.rem(in_head, ROT // 2)
    frequency = jnp.zeros(square, F32)
    for i in range(ROT // 2):
        frequency = jnp.where(pair == i, F32(10000.0 ** (-(2.0 * i) / ROT)), frequency)
    angle = (PREFIX + row_offset).astype(F32) * frequency
    cosine, sine = jnp.cos(angle), jnp.sin(angle)
    lower = in_head < ROT // 2
    upper = (in_head >= ROT // 2) & (in_head < ROT)
    rot_same = jnp.where(in_head < ROT, cosine, 1.0)
    rot_up = jnp.where(lower, -sine, 0.0)
    rot_down = jnp.where(upper, sine, 0.0)

    def rotary(x):
        return (
            x * rot_same
            + pltpu.roll(x, 128 - ROT // 2, 1) * rot_up
            + pltpu.roll(x, ROT // 2, 1) * rot_down
        )

    service(1)

    def normalise(blocks, gain):
        total = jnp.zeros(square, F32)
        for j in range(N_MP):
            total = total + blocks[j].astype(F32)
        mean = jnp.sum(total, axis=1, keepdims=True) / (N_MP * 128)
        squares = jnp.zeros(square, F32)
        for j in range(N_MP):
            centred = blocks[j].astype(F32) - mean
            squares = squares + centred * centred
        scale = lax.rsqrt(jnp.sum(squares, axis=1, keepdims=True) / (N_MP * 128) + EPS)
        for j in range(N_MP):
            centred = blocks[j].astype(F32) - mean
            nrm[:, pl.ds(j * 128, 128)] = (
                centred * scale * gain[pl.ds(j, 1), :].astype(F32)
            ).astype(BF16)

    for n in near_first:
        landed(n, lambda peer: tok, xf, ag1_s, ag1_r)
    get_ga.wait()
    normalise(xf, gain_a)
    for copy in get_qkv:
        copy.wait()
    projected = dot(nrm[...], wqkv[...])
    query = rotary(projected[:, 0:128]).astype(BF16) * BF16(HEAD_DIM ** -0.5)
    keys = rotary(projected[:, 128:256]).astype(BF16)
    values = projected[:, 256:384].astype(BF16)

    zero = jnp.zeros(square, BF16)
    in_group = [(row_group == g) for g in range(2)]
    state = []
    for h in range(2):
        masked = jnp.where((lane // HEAD_DIM) == h, query, zero)
        for g in range(2):
            q2[pl.ds(h * 128, 128), pl.ds(g * 128, 128)] = jnp.where(in_group[g], masked, zero)
        scores = jnp.where(allowed, dot(masked, keys, ((1,), (1,))), NEG)
        top = jnp.max(scores, axis=1, keepdims=True)
        weights = jnp.exp(scores - top)
        mixed = dot(weights.astype(BF16), values)
        for g in range(2):
            acc[pl.ds(h * 128, 128), pl.ds(g * 128, 128)] = jnp.where(in_group[g], mixed, 0.0)
        state.append((top, jnp.sum(weights, axis=1, keepdims=True)))

    def attend(slots):
        for h in range(2):
            top, total = state[h]
            here = pl.ds(h * 128, 128)
            q = q2[here, :]
            scores = [dot(q, kv[slot, 0]) for slot in slots]
            best = functools.reduce(jnp.maximum, scores)
            new_top = jnp.maximum(top, jnp.max(best, axis=1, keepdims=True))
            scale = jnp.exp(top - new_top)
            weights = [jnp.exp(s - new_top) for s in scores]
            total = total * scale + jnp.sum(functools.reduce(jnp.add, weights), axis=1, keepdims=True)
            mixed = acc[here, :] * scale
            for w, slot in zip(weights, slots):
                mixed = mixed + dot(w.astype(BF16), kv[slot, 1])
            acc[here, :] = mixed
            state[h] = (new_top, total)

    def from_pair(pos, step, parts=(0, 1)):
        for part in parts:
            pair_landed(pos, at_z(step), part).wait_recv()

    def both(step):
        slot = at_z(step)
        return [slot, slot + 1 - 2 * core]

    from_pair(0, 0)
    attend(both(0))
    for hop in range(1, 4):
        service(hop + 1)
        from_pair(hop, -hop)
        from_pair(4 + hop, hop)
        attend(both(-hop) + both(hop))
    from_pair(4, -4, (0,))
    from_pair(8, 4, (1,))
    attend(both(4))

    finals = []
    for h in range(2):
        here = pl.ds(h * 128, 128)
        mixed = jnp.where(in_group[0], acc[here, pl.ds(0, 128)], acc[here, pl.ds(128, 128)])
        finals.append(mixed / state[h][1])
    attn_rows = jnp.where(lane < HEAD_DIM, finals[0], finals[1]).astype(BF16)

    get_out.wait()
    for j in range(N_MP // 2):
        share_pair = dot(attn_rows, wout[:, pl.ds(j * 256, 256)]).astype(BF16)
        p1s[2 * j] = share_pair[:, 0:128]
        p1s[2 * j + 1] = share_pair[:, 128:256]
    share(lambda peer: p1s.at[peer], p1r, rs1_s, rs1_r)
    attn_sum = p1s[mp].astype(F32)
    for n in near_first:
        landed(n, lambda peer: p1s.at[peer], p1r, rs1_s, rs1_r)
        attn_sum = attn_sum + p1r[sources[n]].astype(F32)
    residual = (tok[...].astype(F32) + attn_sum).astype(BF16)
    res[...] = residual
    rf[mp] = residual
    share(lambda peer: res, rf, ag2_s, ag2_r)
    get_gm.wait()
    get_gu.wait()
    get_down.wait()
    for n in near_first:
        landed(n, lambda peer: res, rf, ag2_s, ag2_r)

    normalise(rf, gain_m)
    gate_up = dot(wgu[...], nrm[...], ((1,), (1,)))
    units = wdown.shape[0]
    gate, up = gate_up[0:units], gate_up[units:]
    hidden = (gate / (1.0 + jnp.exp(-gate)) * up).astype(BF16)
    for j in range(N_MP // 2):
        share_pair = dot(hidden, wdown[:, pl.ds(j * 256, 256)], ((0,), (0,))).astype(BF16)
        p2s[2 * j] = share_pair[:, 0:128]
        p2s[2 * j + 1] = share_pair[:, 128:256]
    share(lambda peer: p2s.at[peer], p2r, rs2_s, rs2_r)
    mlp_sum = p2s[mp].astype(F32)
    for n in near_first:
        landed(n, lambda peer: p2s.at[peer], p2r, rs2_s, rs2_r)
        mlp_sum = mlp_sum + p2r[sources[n]].astype(F32)
    out_ref[...] = (res[...].astype(F32) + mlp_sum).astype(BF16)
    for copy in sent:
        copy.wait_send()


def body(
    tokens_in, req_lengths, req_groups, prefix_cache, attn_gain, mlp_gain, w_qkv, w_out, w_gate_up, w_down
):
    width = tokens_in.shape[1]
    model_width = w_qkv.shape[0]
    units = w_down.shape[0]
    rows = prefix_cache.shape[1]
    blocks = (N_MP, 128, 128)
    anywhere = pl.BlockSpec(memory_space=pl.ANY)
    scalars = pl.BlockSpec(memory_space=pltpu.SMEM)
    dma = pltpu.SemaphoreType.DMA
    return pl.pallas_call(
        layer_kernel,
        out_shape=jax.ShapeDtypeStruct(tokens_in.shape, BF16),
        in_specs=[scalars, scalars] + [anywhere] * 8,
        out_specs=pl.BlockSpec(memory_space=pltpu.VMEM),
        scratch_shapes=[
            pltpu.VMEM(tokens_in.shape, BF16),
            pltpu.VMEM((4 * rows, width), BF16),
            pltpu.VMEM((N_MP, 128), BF16),
            pltpu.VMEM((N_MP, 128), BF16),
            pltpu.VMEM((model_width, 384), BF16),
            pltpu.VMEM((width, model_width), BF16),
            pltpu.VMEM((2 * units, model_width), BF16),
            pltpu.VMEM((units, model_width), BF16),
            pltpu.VMEM(blocks, BF16),
            pltpu.VMEM((2 * N_Z, 2, rows, 256), BF16),
            pltpu.VMEM((128, model_width), BF16),
            pltpu.VMEM(blocks, BF16),
            pltpu.VMEM(blocks, BF16),
            pltpu.VMEM((128, 128), BF16),
            pltpu.VMEM(blocks, BF16),
            pltpu.VMEM(blocks, BF16),
            pltpu.VMEM(blocks, BF16),
            pltpu.VMEM((256, 256), BF16),
            pltpu.VMEM((256, 256), F32),
            dma((10,)),
        ]
        + [dma((15,))] * 8
        + [dma((16,)), dma((16,)), dma((18,)), dma((18,))],
        compiler_params=pltpu.CompilerParams(
            collective_id=0, has_side_effects=True, vmem_limit_bytes=60 * 1024 * 1024
        ),
        name="layer",
    )(
        req_lengths.T,
        req_groups.T,
        tokens_in,
        prefix_cache.reshape(4 * rows, width),
        attn_gain.reshape(N_MP, 128),
        mlp_gain.reshape(N_MP, 128),
        jnp.transpose(w_qkv, (1, 0, 2)),
        w_out,
        jnp.transpose(w_gate_up, (1, 2, 0)).reshape(2 * units, model_width),
        w_down,
    )


def solution(mesh):
    return jax.shard_map(
        body,
        mesh=mesh,
        in_specs=(
            P("req", "mp"),
            P(),
            P(),
            P(None, "req", None, "mp"),
            P(),
            P(),
            P(None, None, "mp"),
            P("mp", None),
            P(None, None, "mp"),
            P("mp", None),
        ),
        out_specs=P("req", "mp"),
        check_vma=False,
    )
```

time: 392 us -> 65.7 us (0.17)
  waiting for transfers between devices: 192 us -> 0 us
  blocking collectives: 68.4 us -> 0 us
  Pallas kernels: 0 us -> 64.1 us
  matrix products: 55.5 us -> 0 us
  local copies, waits for them, and re-layouts: 54.7 us -> 1.38 us
  between operations: 13.3 us -> 0.01 us
  other arithmetic: 6.08 us -> 0 us
    unnamed x5 -> x0, waiting for transfers between devices: 165 us -> none
    pallas_call x0 -> x1, Pallas kernels: none -> 64.1 us  [body(): pl.pallas_call(layer_kernel, out_shape=jax.ShapeDtypeStruct(tokens_in.sha...]
    dot_general x38 -> x0, matrix products: 55.5 us -> none  [the longest x16 31.8 us: rounded_block(): jnp.einsum('hts,she->the', weights.astype(jnp.bfloat16), value_part, pref...]
    all_gather x2 -> x0, blocking collectives: 37.4 us -> none  [the longest x1 21 us: body(): full_rows = lax.all_gather(tokens_in, 'mp', axis=1, tiled=True)]
    psum x1 -> x0, blocking collectives: 30.9 us -> none  [body(): lax.psum((jnp.sum(residual_f, axis=1), jnp.sum(residual_f * residual_f, a...]
    slice x34 -> x0, local copies, waits for them, and re-layouts: 28.3 us -> none  [the longest x16 26.1 us: rounded_block(): key_part = part[:, :, 0].reshape(group_count, block, heads, HEAD_DIM)]
    all_gather x1 -> x0, waiting for transfers between devices: 26.7 us -> none  [body(): piece = lax.all_gather(prefix_cache, 'req', axis=1, tiled=True)]
    reshape x16 -> x0, local copies, waits for them, and re-layouts: 16 us -> none  [rounded_block(): jnp.where(member[None, :, :, None], scores, NEG)]
  transfers between devices with their start and end apart: 3 -> 0, of which waited for: 3 -> 0; matrix products, arithmetic and copies ran while one was open for 2% -> 0% of each run, Pallas kernels for 0% -> 0%
where the time goes in v1:
time: 65.7 us; the launch traced here: 65.5 us
  Pallas kernels  64.1 us (98%)
  local copies, waits for them, and re-layouts  1.38 us (2%)
    pallas_call x1, Pallas kernels, body(): pl.pallas_call(layer_kernel, out_shape=jax.ShapeDtypeStruct(tokens_in.sha...  64.1 us
    unnamed x1, local copies, waits for them, and re-layouts  1.38 us

profile of v1, /device:TPU:1, one launch (start us, length us, event | category | flops | bytes accessed | tf_op | source)
XLA Modules:
  0.0 65.5 jit_solution(991037099160548401)
XLA Ops:
  0.0 64.1 %layer.1 = bf16[128,128]{1,0:T(8,128)(2,1)} custom-call(s32[4,16]{1,0:T(4,128)} %bitcast.14, s32[4,16]{1,0:T(4,128)} %bitcast.15, bf16[128,128]{1,0:T(8,128)(2,1)} %tokens_hbm.1, bf16[1024,128]{1,0:T(8,128)(2,1)} %bitcast.11, bf16[16,128]{1,0:T(8,128)(2,1)} %bitcast.12, bf16[16,128]{1,0:T(8,128)(2,1)} %bitcast.13, bf16[3,2048,128]{2,1,0:T(8,128)(2,1)} %bitcast.10, ...), custom_call_target="tpu_custom_call" | custom-call | tf_op jit(solution)/shard_map/layer/pallas_call | solution.py:347
  64.1 1.4 %copy.12 = bf16[128,128]{1,0:T(8,128)(2,1)} copy(bf16[128,128]{1,0:T(8,128)(2,1)} %layer.1) | data formatting | bytes 65536

commit v2 on v1

--- a/solution.py
+++ b/solution.py
@@ -17,6 +17,7 @@
 N_MP = 16
 N_Z = 8
 SIDE = 4
+HALF = 64
 OFFSETS = sorted(
     [(dx, dy) for dx in range(SIDE) for dy in range(SIDE) if (dx, dy) != (0, 0)],
     key=lambda o: (-(min(o[0], SIDE - o[0]) + min(o[1], SIDE - o[1])), o),
@@ -129,26 +130,31 @@
         copy.start()
         sent.append(copy)
 
-    def share(src_of, dst, send_sem, recv_sem):
+    def span(half):
+        return pl.ds(half * HALF, HALF)
+
+    def exchange(half, src_of, dst, send_sem, recv_sem, n):
+        index = half * len(OFFSETS) + n
+        return lambda peer, slot: pltpu.make_async_remote_copy(
+            src_ref=src_of(peer).at[span(half)], dst_ref=dst.at[slot, span(half)],
+            send_sem=send_sem.at[index], recv_sem=recv_sem.at[index],
+            device_id={"mp": peer},
+        )
+
+    def share(half, src_of, dst, send_sem, recv_sem):
         for n, peer in enumerate(peers):
-            copy = pltpu.make_async_remote_copy(
-                src_ref=src_of(peer), dst_ref=dst.at[mp],
-                send_sem=send_sem.at[n], recv_sem=recv_sem.at[n],
-                device_id={"mp": peer},
-            )
+            copy = exchange(half, src_of, dst, send_sem, recv_sem, n)(peer, mp)
             copy.start()
             sent.append(copy)
 
-    def landed(n, src_of, dst, send_sem, recv_sem):
-        pltpu.make_async_remote_copy(
-            src_ref=src_of(peers[n]), dst_ref=dst.at[sources[n]],
-            send_sem=send_sem.at[n], recv_sem=recv_sem.at[n],
-            device_id={"mp": peers[n]},
-        ).wait_recv()
+    def landed(half, n, src_of, dst, send_sem, recv_sem):
+        exchange(half, src_of, dst, send_sem, recv_sem, n)(peers[n], sources[n]).wait_recv()
 
     near_first = list(reversed(range(len(OFFSETS))))
 
-    share(lambda peer: tok, xf, ag1_s, ag1_r)
+    gather_in = (lambda peer: tok, xf, ag1_s, ag1_r)
+    for half in range(2):
+        share(half, *gather_in)
 
     def service(hop):
         for way, part in ((0, 0), (1, 1), (0, 1), (1, 0)):
@@ -209,26 +215,28 @@
 
     service(1)
 
-    def normalise(blocks, gain):
-        total = jnp.zeros(square, F32)
+    def normalise(blocks, gain, first, count):
+        here = pl.ds(first, count)
+        total = jnp.zeros((count, 128), F32)
         for j in range(N_MP):
-            total = total + blocks[j].astype(F32)
+            total = total + blocks[j, here].astype(F32)
         mean = jnp.sum(total, axis=1, keepdims=True) / (N_MP * 128)
-        squares = jnp.zeros(square, F32)
+        squares = jnp.zeros((count, 128), F32)
         for j in range(N_MP):
-            centred = blocks[j].astype(F32) - mean
+            centred = blocks[j, here].astype(F32) - mean
             squares = squares + centred * centred
         scale = lax.rsqrt(jnp.sum(squares, axis=1, keepdims=True) / (N_MP * 128) + EPS)
         for j in range(N_MP):
-            centred = blocks[j].astype(F32) - mean
-            nrm[:, pl.ds(j * 128, 128)] = (
+            centred = blocks[j, here].astype(F32) - mean
+            nrm[here, pl.ds(j * 128, 128)] = (
                 centred * scale * gain[pl.ds(j, 1), :].astype(F32)
             ).astype(BF16)
 
-    for n in near_first:
-        landed(n, lambda peer: tok, xf, ag1_s, ag1_r)
+    for half in range(2):
+        for n in near_first:
+            landed(half, n, *gather_in)
     get_ga.wait()
-    normalise(xf, gain_a)
+    normalise(xf, gain_a, 0, 128)
     for copy in get_qkv:
         copy.wait()
     projected = dot(nrm[...], wqkv[...])
@@ -294,41 +302,51 @@
         finals.append(mixed / state[h][1])
     attn_rows = jnp.where(lane < HEAD_DIM, finals[0], finals[1]).astype(BF16)
 
+    scatter_attn = (lambda peer: p1s.at[peer], p1r, rs1_s, rs1_r)
+    gather_mlp = (lambda peer: res, rf, ag2_s, ag2_r)
+    scatter_mlp = (lambda peer: p2s.at[peer], p2r, rs2_s, rs2_r)
+
+    def summed(half, own, exchange_of):
+        total = own[mp, span(half)].astype(F32)
+        for n in near_first:
+            landed(half, n, *exchange_of)
+            total = total + exchange_of[1][sources[n], span(half)].astype(F32)
+        return total
+
     get_out.wait()
-    for j in range(N_MP // 2):
-        share_pair = dot(attn_rows, wout[:, pl.ds(j * 256, 256)]).astype(BF16)
-        p1s[2 * j] = share_pair[:, 0:128]
-        p1s[2 * j + 1] = share_pair[:, 128:256]
-    share(lambda peer: p1s.at[peer], p1r, rs1_s, rs1_r)
-    attn_sum = p1s[mp].astype(F32)
-    for n in near_first:
-        landed(n, lambda peer: p1s.at[peer], p1r, rs1_s, rs1_r)
-        attn_sum = attn_sum + p1r[sources[n]].astype(F32)
-    residual = (tok[...].astype(F32) + attn_sum).astype(BF16)
-    res[...] = residual
-    rf[mp] = residual
-    share(lambda peer: res, rf, ag2_s, ag2_r)
+    for half in range(2):
+        some_rows = attn_rows[half * HALF : (half + 1) * HALF]
+        for j in range(N_MP // 2):
+            share_pair = dot(some_rows, wout[:, pl.ds(j * 256, 256)]).astype(BF16)
+            p1s[2 * j, span(half)] = share_pair[:, 0:128]
+            p1s[2 * j + 1, span(half)] = share_pair[:, 128:256]
+        share(half, *scatter_attn)
     get_gm.wait()
     get_gu.wait()
     get_down.wait()
-    for n in near_first:
-        landed(n, lambda peer: res, rf, ag2_s, ag2_r)
-
-    normalise(rf, gain_m)
-    gate_up = dot(wgu[...], nrm[...], ((1,), (1,)))
+    for half in range(2):
+        attn_sum = summed(half, p1s, scatter_attn)
+        residual = (tok[span(half)].astype(F32) + attn_sum).astype(BF16)
+        res[span(half)] = residual
+        rf[mp, span(half)] = residual
+        share(half, *gather_mlp)
+
     units = wdown.shape[0]
-    gate, up = gate_up[0:units], gate_up[units:]
-    hidden = (gate / (1.0 + jnp.exp(-gate)) * up).astype(BF16)
-    for j in range(N_MP // 2):
-        share_pair = dot(hidden, wdown[:, pl.ds(j * 256, 256)], ((0,), (0,))).astype(BF16)
-        p2s[2 * j] = share_pair[:, 0:128]
-        p2s[2 * j + 1] = share_pair[:, 128:256]
-    share(lambda peer: p2s.at[peer], p2r, rs2_s, rs2_r)
-    mlp_sum = p2s[mp].astype(F32)
-    for n in near_first:
-        landed(n, lambda peer: p2s.at[peer], p2r, rs2_s, rs2_r)
-        mlp_sum = mlp_sum + p2r[sources[n]].astype(F32)
-    out_ref[...] = (res[...].astype(F32) + mlp_sum).astype(BF16)
+    for half in range(2):
+        for n in near_first:
+            landed(half, n, *gather_mlp)
+        normalise(rf, gain_m, half * HALF, HALF)
+        gate_up = dot(wgu[...], nrm[span(half)], ((1,), (1,)))
+        gate, up = gate_up[0:units], gate_up[units:]
+        hidden = (gate / (1.0 + jnp.exp(-gate)) * up).astype(BF16)
+        for j in range(N_MP // 2):
+            share_pair = dot(hidden, wdown[:, pl.ds(j * 256, 256)], ((0,), (0,))).astype(BF16)
+            p2s[2 * j, span(half)] = share_pair[:, 0:128]
+            p2s[2 * j + 1, span(half)] = share_pair[:, 128:256]
+        share(half, *scatter_mlp)
+    for half in range(2):
+        mlp_sum = summed(half, p2s, scatter_mlp)
+        out_ref[span(half)] = (res[span(half)].astype(F32) + mlp_sum).astype(BF16)
     for copy in sent:
         copy.wait_send()
 
@@ -371,7 +389,7 @@
             pltpu.VMEM((256, 256), F32),
             dma((10,)),
         ]
-        + [dma((15,))] * 8
+        + [dma((30,))] * 8
         + [dma((16,)), dma((16,)), dma((18,)), dma((18,))],
         compiler_params=pltpu.CompilerParams(
             collective_id=0, has_side_effects=True, vmem_limit_bytes=60 * 1024 * 1024

time: 65.7 us -> 62.7 us (0.954)
  Pallas kernels: 64.1 us -> 61.2 us
    pallas_call x1, Pallas kernels: 64.1 us -> 61.2 us  [body(): pl.pallas_call(layer_kernel, out_shape=jax.ShapeDtypeStruct(tokens_in.sha...]
where the time goes in v2:
time: 62.7 us; the launch traced here: 62.6 us
  Pallas kernels  61.2 us (98%)
  local copies, waits for them, and re-layouts  1.38 us (2%)
    pallas_call x1, Pallas kernels, body(): pl.pallas_call(layer_kernel, out_shape=jax.ShapeDtypeStruct(tokens_in.sha...  61.2 us
    unnamed x1, local copies, waits for them, and re-layouts  1.38 us

profile of v2, /device:TPU:1, one launch (start us, length us, event | category | flops | bytes accessed | tf_op | source)
XLA Modules:
  0.0 62.6 jit_solution(9331875170027267562)
XLA Ops:
  0.0 61.2 %layer.1 = bf16[128,128]{1,0:T(8,128)(2,1)} custom-call(s32[4,16]{1,0:T(4,128)} %bitcast.14, s32[4,16]{1,0:T(4,128)} %bitcast.15, bf16[128,128]{1,0:T(8,128)(2,1)} %tokens_hbm.1, bf16[1024,128]{1,0:T(8,128)(2,1)} %bitcast.11, bf16[16,128]{1,0:T(8,128)(2,1)} %bitcast.12, bf16[16,128]{1,0:T(8,128)(2,1)} %bitcast.13, bf16[3,2048,128]{2,1,0:T(8,128)(2,1)} %bitcast.10, ...), custom_call_target="tpu_custom_call" | custom-call | tf_op jit(solution)/shard_map/layer/pallas_call | solution.py:365
  61.2 1.4 %copy.12 = bf16[128,128]{1,0:T(8,128)(2,1)} copy(bf16[128,128]{1,0:T(8,128)(2,1)} %layer.1) | data formatting | bytes 65536

commit v3 on v2

v3 whole, which is shorter than its diff:
```python
import functools

import jax
import jax.numpy as jnp
from jax import lax
from jax.experimental import pallas as pl
from jax.experimental.pallas import tpu as pltpu
from jax.sharding import PartitionSpec as P

HEAD_DIM = 64
ROT = 16
PREFIX = 4096
NEG = -1e30
EPS = 1e-05
F32 = jnp.float32
BF16 = jnp.bfloat16
N_MP = 16
N_Z = 8
SIDE = 4
HALF = 64
Z_STEPS = (4, 3, 5, 2, 6, 1, 7)
OFFSETS = sorted(
    [(dx, dy) for dx in range(SIDE) for dy in range(SIDE) if (dx, dy) != (0, 0)],
    key=lambda o: (-(min(o[0], SIDE - o[0]) + min(o[1], SIDE - o[1])), o),
)


def dot(a, b, dims=((1,), (0,))):
    return lax.dot_general(a, b, (dims, ((), ())), preferred_element_type=F32)


def layer_kernel(
    lengths, groups, tokens_hbm, prefix_hbm, gain_a_hbm, gain_m_hbm, wqkv_hbm, wout_hbm, wgu_hbm, wdown_hbm,
    out_ref,
    tok, pre, gain_a, gain_m, wqkv, wout, wgu, wdown,
    xf, kv, nrm, p1s, p1r, res, rf, p2s, p2r, qs, qr, po, pr, so, sr, flip,
    local_sem, ag1_s, ag1_r, rs1_s, rs1_r, ag2_s, ag2_r, rs2_s, rs2_r,
    q_s, q_r, part_s, part_r, stat_s, stat_r, pair_s, pair_r,
):
    mp = lax.axis_index("mp")
    req = lax.axis_index("req")
    z, core = req // 2, req % 2
    mx, my = mp // SIDE, mp % SIDE

    def z_at(step):
        return lax.rem(z + (step + N_Z), N_Z)

    peers = [lax.rem(mx + dx, SIDE) * SIDE + lax.rem(my + dy, SIDE) for dx, dy in OFFSETS]
    sources = [
        lax.rem(mx + SIDE - dx, SIDE) * SIDE + lax.rem(my + SIDE - dy, SIDE) for dx, dy in OFFSETS
    ]
    z_to = [z_at(step) for step in Z_STEPS]
    z_from = [z_at(-step) for step in Z_STEPS]
    partner = z * 2 + (1 - core)

    barrier = pltpu.get_barrier_semaphore()
    pl.semaphore_signal(barrier, inc=1, device_id={"req": partner})
    for there in z_to:
        pl.semaphore_signal(barrier, inc=1, device_id={"req": there * 2 + core})
    for peer in peers:
        pl.semaphore_signal(barrier, inc=1, device_id={"mp": peer})

    def fetch(index, src, dst):
        copy = pltpu.make_async_copy(src, dst, local_sem.at[index])
        copy.start()
        return copy

    get_pre = fetch(0, prefix_hbm, pre)
    get_tok = fetch(1, tokens_hbm, tok)
    get_ga = fetch(2, gain_a_hbm, gain_a)
    get_gm = fetch(3, gain_m_hbm, gain_m)
    get_qkv = [
        fetch(4 + i, wqkv_hbm.at[i], wqkv.at[:, pl.ds(i * 128, 128)]) for i in range(3)
    ]
    get_out = fetch(7, wout_hbm, wout)
    get_gu = fetch(8, wgu_hbm, wgu)
    get_down = fetch(9, wdown_hbm, wdown)

    rows = kv.shape[2]
    get_pre.wait()
    pick_key = (
        lax.broadcasted_iota(jnp.int32, (2 * rows, rows), 0)
        == 2 * lax.broadcasted_iota(jnp.int32, (2 * rows, rows), 1)
    ).astype(F32).astype(BF16)
    pick_value = (
        lax.broadcasted_iota(jnp.int32, (rows, 2 * rows), 1)
        == 2 * lax.broadcasted_iota(jnp.int32, (rows, 2 * rows), 0) + 1
    ).astype(F32).astype(BF16)
    for g in range(2):
        raw = pre[pl.ds(g * 2 * rows, 2 * rows), :]
        kv[core, 0, pl.ds(g * 128, 128), :] = dot(raw, pick_key, ((0,), (0,))).astype(BF16)
        kv[core, 1, :, pl.ds(g * 128, 128)] = dot(pick_value, raw).astype(BF16)
    get_tok.wait()
    xf[mp] = tok[...]

    pl.semaphore_wait(barrier, 1 + len(Z_STEPS) + len(OFFSETS))
    sent = []

    def span(half):
        return pl.ds(half * HALF, HALF)

    def exchange(half, src_of, dst, send_sem, recv_sem, n):
        index = half * len(OFFSETS) + n
        return lambda peer, slot: pltpu.make_async_remote_copy(
            src_ref=src_of(peer).at[span(half)], dst_ref=dst.at[slot, span(half)],
            send_sem=send_sem.at[index], recv_sem=recv_sem.at[index],
            device_id={"mp": peer},
        )

    def share(half, src_of, dst, send_sem, recv_sem):
        for n, peer in enumerate(peers):
            copy = exchange(half, src_of, dst, send_sem, recv_sem, n)(peer, mp)
            copy.start()
            sent.append(copy)

    def landed(half, n, src_of, dst, send_sem, recv_sem):
        exchange(half, src_of, dst, send_sem, recv_sem, n)(peers[n], sources[n]).wait_recv()

    near_first = list(reversed(range(len(OFFSETS))))

    gather_in = (lambda peer: tok, xf, ag1_s, ag1_r)
    for half in range(2):
        share(half, *gather_in)

    def pair_copy(slot):
        return pltpu.make_async_remote_copy(
            src_ref=kv.at[slot], dst_ref=kv.at[slot], send_sem=pair_s, recv_sem=pair_r,
            device_id={"req": partner},
        )

    to_partner = pair_copy(core)
    to_partner.start()
    sent.append(to_partner)

    def z_copy(half, n, src, dst, send_sem, recv_sem, there):
        index = half * len(Z_STEPS) + n
        return pltpu.make_async_remote_copy(
            src_ref=src, dst_ref=dst, send_sem=send_sem.at[index], recv_sem=recv_sem.at[index],
            device_id={"req": there * 2 + core},
        )

    def query_copy(half, n, slot):
        return z_copy(half, n, qs.at[span(half)], qr.at[slot, span(half)], q_s, q_r, z_to[n])

    def part_copy(half, n, slot, there):
        return z_copy(half, n, po.at[there, span(half)], pr.at[slot, span(half)], part_s, part_r, there)

    def stat_copy(half, n, slot, there):
        return z_copy(half, n, so.at[half, there], sr.at[half, slot], stat_s, stat_r, there)

    def meta(shape, axis, first, owner):
        place = lax.broadcasted_iota(jnp.int32, shape, axis) + first
        request = jnp.zeros(shape, jnp.int32)
        start = jnp.zeros(shape, jnp.int32)
        group = jnp.full(shape, groups[0, owner], jnp.int32)
        begin = jnp.int32(0)
        for r in range(1, 4):
            begin = begin + lengths[r - 1, owner]
            inside = place >= begin
            request = request + inside.astype(jnp.int32)
            start = jnp.where(inside, begin, start)
            group = jnp.where(inside, groups[r, owner], group)
        return place, request, place - start, group

    square = (128, 128)
    strip = (HALF, 128)
    row_offset = meta(square, 0, 0, req)[2]
    lane = lax.broadcasted_iota(jnp.int32, square, 1)
    in_head = lax.rem(lane, HEAD_DIM)
    turn = lax.rem(in_head, ROT // 2)
    frequency = jnp.zeros(square, F32)
    for i in range(ROT // 2):
        frequency = jnp.where(turn == i, F32(10000.0 ** (-(2.0 * i) / ROT)), frequency)
    angle = (PREFIX + row_offset).astype(F32) * frequency
    cosine, sine = jnp.cos(angle), jnp.sin(angle)
    lower = in_head < ROT // 2
    upper = (in_head >= ROT // 2) & (in_head < ROT)
    rot_same = jnp.where(in_head < ROT, cosine, 1.0)
    rot_up = jnp.where(lower, -sine, 0.0)
    rot_down = jnp.where(upper, sine, 0.0)
    strip_lane = lax.broadcasted_iota(jnp.int32, strip, 1)
    first_head = strip_lane < HEAD_DIM

    def rotary(x, half):
        here = slice(half * HALF, (half + 1) * HALF)
        return (
            x * rot_same[here]
            + pltpu.roll(x, 128 - ROT // 2, 1) * rot_up[here]
            + pltpu.roll(x, ROT // 2, 1) * rot_down[here]
        )

    def normalise(blocks, gain, first, count):
        here = pl.ds(first, count)
        total = jnp.zeros((count, 128), F32)
        for j in range(N_MP):
            total = total + blocks[j, here].astype(F32)
        mean = jnp.sum(total, axis=1, keepdims=True) / (N_MP * 128)
        squares = jnp.zeros((count, 128), F32)
        for j in range(N_MP):
            centred = blocks[j, here].astype(F32) - mean
            squares = squares + centred * centred
        scale = lax.rsqrt(jnp.sum(squares, axis=1, keepdims=True) / (N_MP * 128) + EPS)
        for j in range(N_MP):
            centred = blocks[j, here].astype(F32) - mean
            nrm[here, pl.ds(j * 128, 128)] = (
                centred * scale * gain[pl.ds(j, 1), :].astype(F32)
            ).astype(BF16)

    zero = jnp.zeros(strip, BF16)

    def split_heads(query):
        return [jnp.where(first_head, query, zero), jnp.where(first_head, zero, query)]

    def stat_rows(tops, sums):
        columns = jnp.zeros(strip, F32)
        for place, column in enumerate(tops + sums):
            columns = jnp.where(strip_lane == place, column, columns)
        turned = jnp.transpose(columns)[0:8]
        return jnp.concatenate([turned, turned], axis=1)

    def chip_part(half, query, owner):
        group = meta(strip, 0, half * HALF, owner)[3]
        wide = []
        for masked in split_heads(query):
            wide.append(
                jnp.concatenate(
                    [jnp.where(group == 0, masked, zero), jnp.where(group == 0, zero, masked)], axis=1
                )
            )
        wide = jnp.concatenate(wide, axis=0)
        scores = [dot(wide, kv[c, 0]) for c in range(2)]
        top = jnp.max(jnp.maximum(scores[0], scores[1]), axis=1, keepdims=True)
        weights = [jnp.exp(s - top) for s in scores]
        total = jnp.sum(weights[0] + weights[1], axis=1, keepdims=True)
        mixed = dot(weights[0].astype(BF16), kv[0, 1]) + dot(weights[1].astype(BF16), kv[1, 1])
        mixed = jnp.where(
            jnp.concatenate([group, group], axis=0) == 0, mixed[:, 0:128], mixed[:, 128:256]
        ) / total
        part = jnp.where(first_head, mixed[0:HALF], mixed[HALF:]).astype(BF16)
        return part, stat_rows([top[0:HALF], top[HALF:]], [total[0:HALF], total[HALF:]])

    def own_part(half, query, keys, values):
        count = keys.shape[0]
        shape = (HALF, count)
        place, request, _, _ = meta(shape, 0, half * HALF, req)
        key_place, key_request, _, _ = meta(shape, 1, 0, req)
        allowed = (request == key_request) & (key_place <= place)
        tops, sums, mixed = [], [], []
        for masked in split_heads(query):
            scores = jnp.where(allowed, dot(masked, keys, ((1,), (1,))), NEG)
            top = jnp.max(scores, axis=1, keepdims=True)
            weights = jnp.exp(scores - top)
            total = jnp.sum(weights, axis=1, keepdims=True)
            mixed.append(dot(weights.astype(BF16), values) / total)
            tops.append(top)
            sums.append(total)
        return jnp.where(first_head, mixed[0], mixed[1]), stat_rows(tops, sums)

    queries, keys, values = [], [], []
    for half in range(2):
        for n in near_first:
            landed(half, n, *gather_in)
        if half == 0:
            get_ga.wait()
            for copy in get_qkv:
                copy.wait()
        normalise(xf, gain_a, half * HALF, HALF)
        projected = dot(nrm[span(half)], wqkv[...])
        query = rotary(projected[:, 0:128], half).astype(BF16) * BF16(HEAD_DIM ** -0.5)
        qs[span(half)] = query
        for n in range(len(Z_STEPS)):
            copy = query_copy(half, n, z)
            copy.start()
            sent.append(copy)
        queries.append(query)
        keys.append(rotary(projected[:, 128:256], half).astype(BF16))
        values.append(projected[:, 256:384].astype(BF16))

    pair_copy(1 - core).wait_recv()
    own = [own_part(0, queries[0], keys[0], values[0])]
    own.append(own_part(1, queries[1], jnp.concatenate(keys, axis=0), jnp.concatenate(values, axis=0)))
    z_order = list(reversed(range(len(Z_STEPS))))
    for half in range(2):
        part, stat = chip_part(half, queries[half], req)
        pr[z, span(half)] = part
        sr[half, z] = stat
        for n in z_order:
            query_copy(half, n, z_from[n]).wait_recv()
            there = z_from[n]
            part, stat = chip_part(half, qr[there, span(half)], there * 2 + core)
            po[there, span(half)] = part
            so[half, there] = stat
            for copy in (stat_copy(half, n, z, there), part_copy(half, n, z, there)):
                copy.start()
                sent.append(copy)

    def attended(half):
        for n in range(len(Z_STEPS)):
            stat_copy(half, n, z_to[n], z_from[n]).wait_recv()
            part_copy(half, n, z_to[n], z_from[n]).wait_recv()
        stats = [sr[half, j] for j in range(N_Z)] + [own[half][1]]
        top = functools.reduce(jnp.maximum, stats)
        scaled = [jnp.exp(stat - top) * pltpu.roll(stat, 6, 0) for stat in stats]
        total = functools.reduce(jnp.add, scaled)
        total = jnp.where(lax.broadcasted_iota(jnp.int32, total.shape, 0) < 2, total, 1.0)
        for j, weight in enumerate(scaled):
            flip[pl.ds(j * 8, 8)] = weight / total
        columns = jnp.transpose(flip[...])[0:HALF]
        result = jnp.zeros(strip, F32)
        for j in range(N_Z + 1):
            part = own[half][0] if j == N_Z else pr[j, span(half)].astype(F32)
            weight = jnp.where(first_head, columns[:, j * 8 : j * 8 + 1], columns[:, j * 8 + 1 : j * 8 + 2])
            result = result + part * weight
        return result.astype(BF16)

    scatter_attn = (lambda peer: p1s.at[peer], p1r, rs1_s, rs1_r)
    gather_mlp = (lambda peer: res, rf, ag2_s, ag2_r)
    scatter_mlp = (lambda peer: p2s.at[peer], p2r, rs2_s, rs2_r)

    def summed(half, own, exchange_of):
        total = own[mp, span(half)].astype(F32)
        for n in near_first:
            landed(half, n, *exchange_of)
            total = total + exchange_of[1][sources[n], span(half)].astype(F32)
        return total

    get_out.wait()
    flip[...] = jnp.zeros_like(flip)
    for half in range(2):
        some_rows = attended(half)
        for j in range(N_MP // 2):
            share_pair = dot(some_rows, wout[:, pl.ds(j * 256, 256)]).astype(BF16)
            p1s[2 * j, span(half)] = share_pair[:, 0:128]
            p1s[2 * j + 1, span(half)] = share_pair[:, 128:256]
        share(half, *scatter_attn)
    get_gm.wait()
    get_gu.wait()
    get_down.wait()
    for half in range(2):
        attn_sum = summed(half, p1s, scatter_attn)
        residual = (tok[span(half)].astype(F32) + attn_sum).astype(BF16)
        res[span(half)] = residual
        rf[mp, span(half)] = residual
        share(half, *gather_mlp)

    units = wdown.shape[0]
    for half in range(2):
        for n in near_first:
            landed(half, n, *gather_mlp)
        normalise(rf, gain_m, half * HALF, HALF)
        gate_up = dot(wgu[...], nrm[span(half)], ((1,), (1,)))
        gate, up = gate_up[0:units], gate_up[units:]
        hidden = (gate / (1.0 + jnp.exp(-gate)) * up).astype(BF16)
        for j in range(N_MP // 2):
            share_pair = dot(hidden, wdown[:, pl.ds(j * 256, 256)], ((0,), (0,))).astype(BF16)
            p2s[2 * j, span(half)] = share_pair[:, 0:128]
            p2s[2 * j + 1, span(half)] = share_pair[:, 128:256]
        share(half, *scatter_mlp)
    for half in range(2):
        mlp_sum = summed(half, p2s, scatter_mlp)
        out_ref[span(half)] = (res[span(half)].astype(F32) + mlp_sum).astype(BF16)
    for copy in sent:
        copy.wait_send()


def body(
    tokens_in, req_lengths, req_groups, prefix_cache, attn_gain, mlp_gain, w_qkv, w_out, w_gate_up, w_down
):
    width = tokens_in.shape[1]
    model_width = w_qkv.shape[0]
    units = w_down.shape[0]
    rows = prefix_cache.shape[1]
    blocks = (N_MP, 128, 128)
    z_blocks = (N_Z, 128, 128)
    anywhere = pl.BlockSpec(memory_space=pl.ANY)
    scalars = pl.BlockSpec(memory_space=pltpu.SMEM)
    dma = pltpu.SemaphoreType.DMA
    return pl.pallas_call(
        layer_kernel,
        out_shape=jax.ShapeDtypeStruct(tokens_in.shape, BF16),
        in_specs=[scalars, scalars] + [anywhere] * 8,
        out_specs=pl.BlockSpec(memory_space=pltpu.VMEM),
        scratch_shapes=[
            pltpu.VMEM(tokens_in.shape, BF16),
            pltpu.VMEM((4 * rows, width), BF16),
            pltpu.VMEM((N_MP, 128), BF16),
            pltpu.VMEM((N_MP, 128), BF16),
            pltpu.VMEM((model_width, 384), BF16),
            pltpu.VMEM((width, model_width), BF16),
            pltpu.VMEM((2 * units, model_width), BF16),
            pltpu.VMEM((units, model_width), BF16),
            pltpu.VMEM(blocks, BF16),
            pltpu.VMEM((2, 2, rows, 256), BF16),
            pltpu.VMEM((128, model_width), BF16),
            pltpu.VMEM(blocks, BF16),
            pltpu.VMEM(blocks, BF16),
            pltpu.VMEM((128, 128), BF16),
            pltpu.VMEM(blocks, BF16),
            pltpu.VMEM(blocks, BF16),
            pltpu.VMEM(blocks, BF16),
            pltpu.VMEM((128, 128), BF16),
            pltpu.VMEM(z_blocks, BF16),
            pltpu.VMEM(z_blocks, BF16),
            pltpu.VMEM(z_blocks, BF16),
            pltpu.VMEM((2, N_Z, 8, 128), F32),
            pltpu.VMEM((2, N_Z, 8, 128), F32),
            pltpu.VMEM((128, 128), F32),
            dma((10,)),
        ]
        + [dma((30,))] * 8
        + [dma((14,))] * 6
        + [dma] * 2,
        compiler_params=pltpu.CompilerParams(
            collective_id=0, has_side_effects=True, vmem_limit_bytes=60 * 1024 * 1024
        ),
        name="layer",
    )(
        req_lengths.T,
        req_groups.T,
        tokens_in,
        prefix_cache.reshape(4 * rows, width),
        attn_gain.reshape(N_MP, 128),
        mlp_gain.reshape(N_MP, 128),
        jnp.transpose(w_qkv, (1, 0, 2)),
        w_out,
        jnp.transpose(w_gate_up, (1, 2, 0)).reshape(2 * units, model_width),
        w_down,
    )


def solution(mesh):
    return jax.shard_map(
        body,
        mesh=mesh,
        in_specs=(
            P("req", "mp"),
            P(),
            P(),
            P(None, "req", None, "mp"),
            P(),
            P(),
            P(None, None, "mp"),
            P("mp", None),
            P(None, None, "mp"),
            P("mp", None),
        ),
        out_specs=P("req", "mp"),
        check_vma=False,
    )
```

time: 62.7 us -> 60.5 us (0.965)
  the two profiles are of different devices: /device:TPU:1 before, /device:TPU:32 now
where the time goes in v3:
time: 60.5 us; the launch traced here: 60.4 us
  Pallas kernels  59 us (98%)
  local copies, waits for them, and re-layouts  1.38 us (2%)
    pallas_call x1, Pallas kernels, body(): pl.pallas_call(layer_kernel, out_shape=jax.ShapeDtypeStruct(tokens_in.sha...  59 us
    unnamed x1, local copies, waits for them, and re-layouts  1.38 us

profile of v3, /device:TPU:32, one launch (start us, length us, event | category | flops | bytes accessed | tf_op | source)
XLA Modules:
  0.0 60.4 jit_solution(13158950724261846865)
XLA Ops:
  0.0 59.0 %layer.1 = bf16[128,128]{1,0:T(8,128)(2,1)} custom-call(s32[4,16]{1,0:T(4,128)} %bitcast.14, s32[4,16]{1,0:T(4,128)} %bitcast.15, bf16[128,128]{1,0:T(8,128)(2,1)} %tokens_hbm.1, bf16[1024,128]{1,0:T(8,128)(2,1)} %bitcast.11, bf16[16,128]{1,0:T(8,128)(2,1)} %bitcast.12, bf16[16,128]{1,0:T(8,128)(2,1)} %bitcast.13, bf16[3,2048,128]{2,1,0:T(8,128)(2,1)} %bitcast.10, ...), custom_call_target="tpu_custom_call" | custom-call | tf_op jit(solution)/shard_map/layer/pallas_call | solution.py:378
  59.0 1.4 %copy.12 = bf16[128,128]{1,0:T(8,128)(2,1)} copy(bf16[128,128]{1,0:T(8,128)(2,1)} %layer.1) | data formatting | bytes 65536
